TPU v7x, 32 devices: a whole 2x2x4 slice. The times are simulated.
32 devices in a mesh: dp: 2 (over y), fsdp: 16 (over z, x, core).
Axes of the slice: x: 2, y: 2, z: 4, core: 2. Of those that a mesh axis runs over, the one named last changes fastest.
Arguments:
- tokens: bfloat16 [65536, 768], P(('dp', 'fsdp')), may hold values from -12 to 12
- cotangent: bfloat16 [65536, 768], P(('dp', 'fsdp')), may hold values from -12 to 12
- segment_ids: int32 [65536], P(('dp', 'fsdp')), may hold values from 0 to 2687, as said below
- first_gain: bfloat16 [768], P('fsdp'), may hold values from 0.25 to 1.75
- first_shift: bfloat16 [768], P('fsdp'), may hold values from -1.75 to 1.75
- triple_weight: bfloat16 [768, 2304], P('fsdp'), may hold values from -0.3125 to 0.3125
- query_bias: bfloat16 [768], P('fsdp'), may hold values from -3 to 3
- value_bias: bfloat16 [768], P('fsdp'), may hold values from -1.75 to 1.75
- out_weight: bfloat16 [768, 768], P('fsdp'), may hold values from -0.875 to 0.875
- out_bias: bfloat16 [768], P('fsdp'), may hold values from -1.75 to 1.75
- second_gain: bfloat16 [768], P('fsdp'), may hold values from 0.25 to 1.75
- second_shift: bfloat16 [768], P('fsdp'), may hold values from -1.75 to 1.75
- up_weight: bfloat16 [768, 3072], P('fsdp'), may hold values from -0.21875 to 0.21875
- up_bias: bfloat16 [3072], P('fsdp'), may hold values from -3 to 3
- down_weight: bfloat16 [3072, 768], P('fsdp'), may hold values from -0.109375 to 0.109375
- down_bias: bfloat16 [768], P('fsdp'), may hold values from -1.75 to 1.75
Outputs:
- block_output: bfloat16 [65536, 768], P(('dp', 'fsdp'))
- tokens_gradient: bfloat16 [65536, 768], P(('dp', 'fsdp'))
- first_gain_gradient: float32 [768], P('fsdp')
- first_shift_gradient: float32 [768], P('fsdp')
- triple_weight_gradient: float32 [768, 2304], P('fsdp')
- query_bias_gradient: float32 [768], P('fsdp')
- value_bias_gradient: float32 [768], P('fsdp')
- out_weight_gradient: float32 [768, 768], P('fsdp')
- out_bias_gradient: float32 [768], P('fsdp')
- second_gain_gradient: float32 [768], P('fsdp')
- second_shift_gradient: float32 [768], P('fsdp')
- up_weight_gradient: float32 [768, 3072], P('fsdp')
- up_bias_gradient: float32 [3072], P('fsdp')
- down_weight_gradient: float32 [3072, 768], P('fsdp')
- down_bias_gradient: float32 [768], P('fsdp')
Inputs may be any that keep to these rules, and one draw needn't show every extreme that they name: `segment_ids`: segment numbers never fall along the patches and no image spans two aligned blocks of 1024 patches; each image has 900 patches and begins its block, or has 1 to 64 patches; the first block begins with an image of 900 patches; the last patch carries exactly the largest number, 65536 // 1024 * (1024 // max(1, 25) + 2) - 1.
All inputs are finite; a program needn't handle non-finite values.
Results may differ from a plain program's by a relative error of at most 0.014.
Values may be sent and summed in bfloat16 or wider, within the bound.
A program may use at most 384 MiB of HBM per device.

v0:
```python
import jax
import jax.numpy as jnp
from jax import lax
from jax.sharding import PartitionSpec as P

H = 12
HD = 64
ROWS = 1024
MB = 2


norm_eps = 1e-06
root_half = 0.7071067811865476
root_inv_two_pi = 0.3989422804014327


def norm_forward(values, gain, shift):
    mean_val = jnp.mean(values, axis=-1, keepdims=True)
    centered = values - mean_val
    variance = jnp.mean(centered * centered, axis=-1, keepdims=True)
    inv_std = lax.rsqrt(variance + norm_eps)
    normed = centered * inv_std
    return (normed * gain + shift, normed, inv_std)


def norm_backward(grad_out, normed, inv_std, gain):
    gain_part = jnp.sum(grad_out * normed, axis=0)
    shift_part = jnp.sum(grad_out, axis=0)
    grad_norm = grad_out * gain
    mean_plain = jnp.mean(grad_norm, axis=-1, keepdims=True)
    mean_cross = jnp.mean(grad_norm * normed, axis=-1, keepdims=True)
    return (inv_std * (grad_norm - mean_plain - normed * mean_cross), gain_part, shift_part)


def gelu_slope(upped):
    normal_cdf = 0.5 * (1.0 + lax.erf(upped * root_half))
    return normal_cdf + upped * jnp.exp(-0.5 * upped * upped) * root_inv_two_pi


def masked_scores(query_block, keys, seg_block, segments):
    scores = (
        jnp.einsum("qhd,khd->hqk", query_block, keys, preferred_element_type=jnp.float32) * 0.125
    )
    allowed = seg_block[:, None] == segments[None, :]
    return jnp.where(allowed[None], scores, -1e30)


def attend_forward(query, keys, value, segments):
    row_count = query.shape[0]
    block = min(512, row_count)
    pieces = []
    log_totals = []
    for begin in range(0, row_count, block):
        scores = masked_scores(
            query[begin : begin + block], keys, segments[begin : begin + block], segments
        )
        peak = jnp.max(scores, axis=-1, keepdims=True)
        exponent = jnp.exp(scores - peak)
        total = jnp.sum(exponent, axis=-1, keepdims=True)
        soft_low = (exponent / total).astype(jnp.bfloat16)
        pieces.append(
            jnp.einsum("hqk,khd->qhd", soft_low, value, preferred_element_type=jnp.float32)
        )
        log_totals.append(peak[..., 0] + jnp.log(total[..., 0]))
    return (jnp.concatenate(pieces, axis=0), jnp.concatenate(log_totals, axis=1))


def attend_backward(query, keys, value, segments, log_total, grad_mixed):
    row_count = query.shape[0]
    block = min(512, row_count)
    query_grads = []
    key_grad = jnp.zeros(keys.shape, jnp.float32)
    value_grad = jnp.zeros(value.shape, jnp.float32)
    for begin in range(0, row_count, block):
        query_block = query[begin : begin + block]
        grad_block = grad_mixed[begin : begin + block]
        scores = masked_scores(query_block, keys, segments[begin : begin + block], segments)
        soft = jnp.exp(scores - log_total[:, begin : begin + block, None])
        grad_soft = jnp.einsum(
            "qhd,khd->hqk", grad_block, value, preferred_element_type=jnp.float32
        )
        center = jnp.sum(soft * grad_soft, axis=-1, keepdims=True)
        grad_scores = (soft * (grad_soft - center)).astype(jnp.bfloat16)
        query_grads.append(
            jnp.einsum("hqk,khd->qhd", grad_scores, keys, preferred_element_type=jnp.float32)
            * 0.125
        )
        key_grad = (
            key_grad
            + jnp.einsum(
                "hqk,qhd->khd", grad_scores, query_block, preferred_element_type=jnp.float32
            )
            * 0.125
        )
        value_grad = value_grad + jnp.einsum(
            "hqk,qhd->khd",
            soft.astype(jnp.bfloat16),
            grad_block,
            preferred_element_type=jnp.float32,
        )
    return (jnp.concatenate(query_grads, axis=0), key_grad, value_grad)


def layer_forward(full, inputs, segments):
    (
        first_gain,
        first_shift,
        triple_weight,
        query_bias,
        value_bias,
        out_weight,
        out_bias,
        second_gain,
        second_shift,
        up_weight,
        up_bias,
        down_weight,
        down_bias,
    ) = full
    width = out_weight.shape[0]
    values = inputs.astype(jnp.float32)
    first_h, first_n, first_r = norm_forward(
        values, first_gain.astype(jnp.float32), first_shift.astype(jnp.float32)
    )
    first_in = first_h.astype(jnp.bfloat16)
    projected = jnp.dot(first_in, triple_weight, preferred_element_type=jnp.float32)
    query = (
        (projected[:, :width] + query_bias.astype(jnp.float32))
        .astype(jnp.bfloat16)
        .reshape(-1, H, HD)
    )
    keys = projected[:, width : 2 * width].astype(jnp.bfloat16).reshape(-1, H, HD)
    value = (
        (projected[:, 2 * width :] + value_bias.astype(jnp.float32))
        .astype(jnp.bfloat16)
        .reshape(-1, H, HD)
    )
    attended, log_total = attend_forward(query, keys, value, segments)
    mixed = attended.reshape(-1, width).astype(jnp.bfloat16)
    resid = (
        values
        + jnp.dot(mixed, out_weight, preferred_element_type=jnp.float32)
        + out_bias.astype(jnp.float32)
    )
    second_h, second_n, second_r = norm_forward(
        resid, second_gain.astype(jnp.float32), second_shift.astype(jnp.float32)
    )
    second_in = second_h.astype(jnp.bfloat16)
    upped = jnp.dot(second_in, up_weight, preferred_element_type=jnp.float32) + up_bias.astype(
        jnp.float32
    )
    act = jax.nn.gelu(upped, approximate=False).astype(jnp.bfloat16)
    result = (
        resid
        + jnp.dot(act, down_weight, preferred_element_type=jnp.float32)
        + down_bias.astype(jnp.float32)
    )
    saved = (
        first_n,
        first_r,
        first_in,
        query,
        keys,
        value,
        log_total,
        mixed,
        second_n,
        second_r,
        second_in,
        upped,
        act,
    )
    return (result.astype(jnp.bfloat16), saved)


def layer_backward(full, saved, grad_result, segments):
    (
        first_gain,
        first_shift,
        triple_weight,
        query_bias,
        value_bias,
        out_weight,
        out_bias,
        second_gain,
        second_shift,
        up_weight,
        up_bias,
        down_weight,
        down_bias,
    ) = full
    (
        first_n,
        first_r,
        first_in,
        query,
        keys,
        value,
        log_total,
        mixed,
        second_n,
        second_r,
        second_in,
        upped,
        act,
    ) = saved
    width = out_weight.shape[0]
    grad_out = grad_result.astype(jnp.float32)
    down_bias_part = jnp.sum(grad_out, axis=0)
    grad_low = grad_out.astype(jnp.bfloat16)
    down_weight_part = jnp.einsum("rf,rd->fd", act, grad_low, preferred_element_type=jnp.float32)
    grad_act = jnp.einsum("rd,fd->rf", grad_low, down_weight, preferred_element_type=jnp.float32)
    grad_up = grad_act * gelu_slope(upped)
    up_bias_part = jnp.sum(grad_up, axis=0)
    grad_up_low = grad_up.astype(jnp.bfloat16)
    up_weight_part = jnp.einsum(
        "rd,rf->df", second_in, grad_up_low, preferred_element_type=jnp.float32
    )
    grad_second = jnp.einsum(
        "rf,df->rd", grad_up_low, up_weight, preferred_element_type=jnp.float32
    )
    resid_part, second_gain_part, second_shift_part = norm_backward(
        grad_second, second_n, second_r, second_gain.astype(jnp.float32)
    )
    grad_resid = grad_out + resid_part
    out_bias_part = jnp.sum(grad_resid, axis=0)
    resid_low = grad_resid.astype(jnp.bfloat16)
    out_weight_part = jnp.einsum("rd,re->de", mixed, resid_low, preferred_element_type=jnp.float32)
    grad_mixed = jnp.einsum(
        "re,de->rd", resid_low, out_weight, preferred_element_type=jnp.float32
    ).astype(jnp.bfloat16)
    query_grad, key_grad, value_grad = attend_backward(
        query, keys, value, segments, log_total, grad_mixed.reshape(-1, H, HD)
    )
    query_low = query_grad.reshape(-1, width).astype(jnp.bfloat16)
    key_low = key_grad.reshape(-1, width).astype(jnp.bfloat16)
    value_low = value_grad.reshape(-1, width).astype(jnp.bfloat16)
    query_bias_part = jnp.sum(query_low, axis=0, dtype=jnp.float32)
    value_bias_part = jnp.sum(value_low, axis=0, dtype=jnp.float32)
    grad_projected = jnp.concatenate([query_low, key_low, value_low], axis=1)
    triple_weight_part = jnp.einsum(
        "rd,re->de", first_in, grad_projected, preferred_element_type=jnp.float32
    )
    grad_first = jnp.einsum(
        "re,de->rd", grad_projected, triple_weight, preferred_element_type=jnp.float32
    )
    input_part, first_gain_part, first_shift_part = norm_backward(
        grad_first, first_n, first_r, first_gain.astype(jnp.float32)
    )
    grad_inputs = (grad_resid + input_part).astype(jnp.bfloat16)
    parts = (
        first_gain_part,
        first_shift_part,
        triple_weight_part,
        query_bias_part,
        value_bias_part,
        out_weight_part,
        out_bias_part,
        second_gain_part,
        second_shift_part,
        up_weight_part,
        up_bias_part,
        down_weight_part,
        down_bias_part,
    )
    return (grad_inputs, parts)


def on_device(
    tokens,
    cotangent,
    segment_ids,
    first_gain,
    first_shift,
    triple_weight,
    query_bias,
    value_bias,
    out_weight,
    out_bias,
    second_gain,
    second_shift,
    up_weight,
    up_bias,
    down_weight,
    down_bias,
):
    shards = (
        first_gain,
        first_shift,
        triple_weight,
        query_bias,
        value_bias,
        out_weight,
        out_bias,
        second_gain,
        second_shift,
        up_weight,
        up_bias,
        down_weight,
        down_bias,
    )
    totals = tuple((jnp.zeros(piece.shape, jnp.float32) for piece in shards))
    results = []
    input_grads = []
    for micro in range(MB):
        lower = micro * ROWS
        segments = segment_ids[lower : lower + ROWS]
        forward_full = (
            lax.all_gather(first_gain, "fsdp", axis=0, tiled=True),
            lax.all_gather(first_shift, "fsdp", axis=0, tiled=True),
            lax.all_gather(triple_weight, "fsdp", axis=0, tiled=True),
            lax.all_gather(query_bias, "fsdp", axis=0, tiled=True),
            lax.all_gather(value_bias, "fsdp", axis=0, tiled=True),
            lax.all_gather(out_weight, "fsdp", axis=0, tiled=True),
            lax.all_gather(out_bias, "fsdp", axis=0, tiled=True),
            lax.all_gather(second_gain, "fsdp", axis=0, tiled=True),
            lax.all_gather(second_shift, "fsdp", axis=0, tiled=True),
            lax.all_gather(up_weight, "fsdp", axis=0, tiled=True),
            lax.all_gather(up_bias, "fsdp", axis=0, tiled=True),
            lax.all_gather(down_weight, "fsdp", axis=0, tiled=True),
            lax.all_gather(down_bias, "fsdp", axis=0, tiled=True),
        )
        result, saved = layer_forward(forward_full, tokens[lower : lower + ROWS], segments)
        results.append(result)
        backward_full = (
            lax.all_gather(first_gain, "fsdp", axis=0, tiled=True),
            lax.all_gather(first_shift, "fsdp", axis=0, tiled=True),
            lax.all_gather(triple_weight, "fsdp", axis=0, tiled=True),
            lax.all_gather(query_bias, "fsdp", axis=0, tiled=True),
            lax.all_gather(value_bias, "fsdp", axis=0, tiled=True),
            lax.all_gather(out_weight, "fsdp", axis=0, tiled=True),
            lax.all_gather(out_bias, "fsdp", axis=0, tiled=True),
            lax.all_gather(second_gain, "fsdp", axis=0, tiled=True),
            lax.all_gather(second_shift, "fsdp", axis=0, tiled=True),
            lax.all_gather(up_weight, "fsdp", axis=0, tiled=True),
            lax.all_gather(up_bias, "fsdp", axis=0, tiled=True),
            lax.all_gather(down_weight, "fsdp", axis=0, tiled=True),
            lax.all_gather(down_bias, "fsdp", axis=0, tiled=True),
        )
        grad_inputs, parts = layer_backward(
            backward_full, saved, cotangent[lower : lower + ROWS], segments
        )
        input_grads.append(grad_inputs)
        p0, p1, p2, p3, p4, p5, p6, p7, p8, p9, p10, p11, p12 = parts
        summed = (
            lax.psum_scatter(p0, "fsdp", scatter_dimension=0, tiled=True),
            lax.psum_scatter(p1, "fsdp", scatter_dimension=0, tiled=True),
            lax.psum_scatter(p2, "fsdp", scatter_dimension=0, tiled=True),
            lax.psum_scatter(p3, "fsdp", scatter_dimension=0, tiled=True),
            lax.psum_scatter(p4, "fsdp", scatter_dimension=0, tiled=True),
            lax.psum_scatter(p5, "fsdp", scatter_dimension=0, tiled=True),
            lax.psum_scatter(p6, "fsdp", scatter_dimension=0, tiled=True),
            lax.psum_scatter(p7, "fsdp", scatter_dimension=0, tiled=True),
            lax.psum_scatter(p8, "fsdp", scatter_dimension=0, tiled=True),
            lax.psum_scatter(p9, "fsdp", scatter_dimension=0, tiled=True),
            lax.psum_scatter(p10, "fsdp", scatter_dimension=0, tiled=True),
            lax.psum_scatter(p11, "fsdp", scatter_dimension=0, tiled=True),
            lax.psum_scatter(p12, "fsdp", scatter_dimension=0, tiled=True),
        )
        totals = tuple((left + right for left, right in zip(totals, summed)))
    s0, s1, s2, s3, s4, s5, s6, s7, s8, s9, s10, s11, s12 = totals
    final = (
        lax.psum(s0.astype(jnp.bfloat16), "dp").astype(jnp.float32),
        lax.psum(s1.astype(jnp.bfloat16), "dp").astype(jnp.float32),
        lax.psum(s2.astype(jnp.bfloat16), "dp").astype(jnp.float32),
        lax.psum(s3.astype(jnp.bfloat16), "dp").astype(jnp.float32),
        lax.psum(s4.astype(jnp.bfloat16), "dp").astype(jnp.float32),
        lax.psum(s5.astype(jnp.bfloat16), "dp").astype(jnp.float32),
        lax.psum(s6.astype(jnp.bfloat16), "dp").astype(jnp.float32),
        lax.psum(s7.astype(jnp.bfloat16), "dp").astype(jnp.float32),
        lax.psum(s8.astype(jnp.bfloat16), "dp").astype(jnp.float32),
        lax.psum(s9.astype(jnp.bfloat16), "dp").astype(jnp.float32),
        lax.psum(s10.astype(jnp.bfloat16), "dp").astype(jnp.float32),
        lax.psum(s11.astype(jnp.bfloat16), "dp").astype(jnp.float32),
        lax.psum(s12.astype(jnp.bfloat16), "dp").astype(jnp.float32),
    )
    return (
        jnp.concatenate(results, axis=0),
        jnp.concatenate(input_grads, axis=0),
        final[0],
        final[1],
        final[2],
        final[3],
        final[4],
        final[5],
        final[6],
        final[7],
        final[8],
        final[9],
        final[10],
        final[11],
        final[12],
    )


def solution(mesh):
    in_specs = (
        P(("dp", "fsdp"), None),
        P(("dp", "fsdp"), None),
        P(("dp", "fsdp")),
        P("fsdp"),
        P("fsdp"),
        P("fsdp", None),
        P("fsdp"),
        P("fsdp"),
        P("fsdp", None),
        P("fsdp"),
        P("fsdp"),
        P("fsdp"),
        P("fsdp", None),
        P("fsdp"),
        P("fsdp", None),
        P("fsdp"),
    )
    out_specs = (
        P(("dp", "fsdp"), None),
        P(("dp", "fsdp"), None),
        P("fsdp"),
        P("fsdp"),
        P("fsdp", None),
        P("fsdp"),
        P("fsdp"),
        P("fsdp", None),
        P("fsdp"),
        P("fsdp"),
        P("fsdp"),
        P("fsdp", None),
        P("fsdp"),
        P("fsdp", None),
        P("fsdp"),
    )
    return jax.shard_map(
        on_device, mesh=mesh, in_specs=in_specs, out_specs=out_specs, check_vma=False
    )
```

profile of v0, /device:TPU:0, one launch (start us, length us, event | category | flops | bytes accessed | tf_op | source)
XLA Modules:
  0.0 1104.1 jit_solution(5142248432136446658)
XLA Ops:
  21.7 63.5 %all-reduce.19 = (bf16[768]{0:T(1024)(128)(2,1)S(1)}, bf16[768]{0:T(1024)(128)(2,1)S(1)}, bf16[768]{0:T(1024)(128)(2,1)S(1)}, bf16[768]{0:T(1024)(128)(2,1)S(1)}...) all-reduce(bf16[768]{0:T(1024)(128)(2,1)S(1)} %dynamic-update-slice, ...), channel_id=1, replica_groups=mesh['dp'=2,'fsdp'=16] {'fsdp'}, use_global_device_ids=true, to_apply=%add.1 | all-reduce | flops 9216 | bytes 36864
  104.4 7.2 fusion.147
  118.2 7.8 fusion.90
  144.8 12.3 %fusion.55 = (f32[12,512]{1,0:T(8,128)S(1)}, f32[12,512,1024]{2,1,0:T(8,128)}) fusion(pred[512,1024]{1,0:T(8,128)(4,1)} %get-tuple-element.151, bf16[512,12,64]{0,2,1:T(8,128)(2,1)} %bitcast.134, bf16[1024,12,64]{0,2,1:T(8,128)(2,1)S(1)} %bitcast.116), kind=kOutput, calls=%fused_computation.95 | convolution fusion | flops 824174592 | bytes 28073984 | tf_op jit(solution)/shard_map/qhd,khd->hqk/dot_general | solution.py:42
  157.1 12.5 %fusion.1 = f32[12,512]{1,0:T(8,128)S(1)} fusion(f32[12,512]{1,0:T(8,128)S(1)} %get-tuple-element.122, f32[12,512,1024]{2,1,0:T(8,128)} %get-tuple-element.123, pred[512,1024]{1,0:T(8,128)(4,1)} %get-tuple-element.151), kind=kLoop, calls=%fused_computation.25 | loop fusion | flops 25159680 | bytes 25739264 | tf_op jit(solution)/shard_map/reduce_sum | solution.py:59
  173.4 9.4 fusion.113
  182.8 12.1 %fusion.54 = (f32[12,512]{1,0:T(8,128)S(1)}, f32[12,512,1024]{2,1,0:T(8,128)}) fusion(pred[512,1024]{1,0:T(8,128)(4,1)} %get-tuple-element.152, bf16[512,12,64]{0,2,1:T(8,128)(2,1)} %bitcast.136, bf16[1024,12,64]{0,2,1:T(8,128)(2,1)S(1)} %bitcast.117), kind=kOutput, calls=%fused_computation.94 | convolution fusion | flops 824174592 | bytes 28073984 | tf_op jit(solution)/shard_map/qhd,khd->hqk/dot_general | solution.py:42
  194.9 13.6 %fusion = f32[12,512]{1,0:T(8,128)S(1)} fusion(f32[12,512]{1,0:T(8,128)S(1)} %get-tuple-element.124, f32[12,512,1024]{2,1,0:T(8,128)} %get-tuple-element.125, pred[512,1024]{1,0:T(8,128)(4,1)} %get-tuple-element.152), kind=kLoop, calls=%fused_computation.24 | loop fusion | flops 25159680 | bytes 25739264 | tf_op jit(solution)/shard_map/reduce_sum | solution.py:59
  211.2 8.5 fusion.112
  219.8 12.3 %fusion.57 = (f32[12,512]{1,0:T(8,128)S(1)}, f32[12,512,1024]{2,1,0:T(8,128)}) fusion(pred[512,1024]{1,0:T(8,128)(4,1)S(1)} %copy-done.29, bf16[512,12,64]{0,2,1:T(8,128)(2,1)} %bitcast.132, bf16[1024,12,64]{0,2,1:T(8,128)(2,1)S(1)} %bitcast.120), kind=kOutput, calls=%fused_computation.97 | convolution fusion | flops 824174592 | bytes 28073984 | tf_op jit(solution)/shard_map/qhd,khd->hqk/dot_general | solution.py:42
  232.1 12.3 %fusion.3 = f32[12,512]{1,0:T(8,128)S(1)} fusion(f32[12,512]{1,0:T(8,128)S(1)} %get-tuple-element.118, f32[12,512,1024]{2,1,0:T(8,128)} %get-tuple-element.119, pred[512,1024]{1,0:T(8,128)(4,1)S(1)} %copy-done.29), kind=kLoop, calls=%fused_computation.27 | loop fusion | flops 25159680 | bytes 25739264 | tf_op jit(solution)/shard_map/reduce_sum | solution.py:59
  247.5 8.5 fusion.115
  255.9 12.0 %fusion.56 = (f32[12,512]{1,0:T(8,128)S(1)}, f32[12,512,1024]{2,1,0:T(8,128)}) fusion(pred[512,1024]{1,0:T(8,128)(4,1)S(1)} %copy-done.26, bf16[512,12,64]{0,2,1:T(8,128)(2,1)} %bitcast.138, bf16[1024,12,64]{0,2,1:T(8,128)(2,1)S(1)} %bitcast.121), kind=kOutput, calls=%fused_computation.96 | convolution fusion | flops 824174592 | bytes 28073984 | tf_op jit(solution)/shard_map/qhd,khd->hqk/dot_general | solution.py:42
  268.0 12.3 %fusion.2 = f32[12,512]{1,0:T(8,128)S(1)} fusion(f32[12,512]{1,0:T(8,128)S(1)} %get-tuple-element.120, f32[12,512,1024]{2,1,0:T(8,128)} %get-tuple-element.121, pred[512,1024]{1,0:T(8,128)(4,1)S(1)} %copy-done.26), kind=kLoop, calls=%fused_computation.26 | loop fusion | flops 25159680 | bytes 25739264 | tf_op jit(solution)/shard_map/reduce_sum | solution.py:59
  284.1 8.0 fusion.114
  304.6 11.0 fusion.153
  315.6 13.5 %fusion.166 = (f32[3072]{0:T(1024)}, bf16[1024,3072]{1,0:T(8,128)(2,1)S(1)}) fusion(f32[1024,3072]{1,0:T(8,128)} %fusion.153, f32[3072]{0:T(1024)S(1)} %copy-done.99, bf16[3072,768]{1,0:T(8,128)(2,1)} %all-gather.11.cloned.1.call-done, bf16[2048,768]{1,0:T(8,128)(2,1)} %param.17), kind=kOutput, calls=%fused_computation.289 | convolution fusion | flops 4869583872 | bytes 25190400 | tf_op jit(solution)/shard_map/rd,fd->rf/dot_general | solution.py:212
  335.8 61.5 %fusion.10 = (bf16[1024,3072]{1,0:T(8,128)(2,1)}, bf16[1024,3072]{1,0:T(8,128)(2,1)}, f32[1024,3072]{1,0:T(8,128)}) fusion(f32[3072]{0:T(1024)S(1)} %copy-done.99, f32[1024,3072]{1,0:T(8,128)S(1)} %bitcast.165, bf16[768,3072]{1,0:T(8,128)(2,1)S(1)} %copy-done.110, f32[1024,768]{1,0:T(8,128)S(1)} %get-tuple-element.127, f32[768]{0:T(1024)S(1)} %copy-done.64, ...), kind=kOutput, calls=%fused_computation.38 | convolution fusion | flops 5251006464 | bytes 45639680 | tf_op jit(solution)/shard_map/dot_general | solution.py:149
  397.4 12.0 %fusion.165 = (f32[3072]{0:T(1024)}, bf16[1024,3072]{1,0:T(8,128)(2,1)S(1)}) fusion(f32[1024,3072]{1,0:T(8,128)} %get-tuple-element.130, f32[3072]{0:T(1024)S(1)} %copy-done.99, bf16[3072,768]{1,0:T(8,128)(2,1)} %all-gather.11.cloned.1.call-done, bf16[2048,768]{1,0:T(8,128)(2,1)S(1)} %copy-done.48), kind=kOutput, calls=%fused_computation.288 | convolution fusion | flops 4869583872 | bytes 25190400 | tf_op jit(solution)/shard_map/rd,fd->rf/dot_general | solution.py:212
  409.4 12.9 %multiply_reduce_fusion.5 = (f32[768]{0:T(1024)}, f32[1024]{0:T(1024)S(1)}, f32[1024]{0:T(1024)S(1)}, f32[768]{0:T(1024)}, f32[768]{0:T(1024)}, /*index=5*/f32[1...) fusion(f32[1024,768]{1,0:T(8,128)S(1)} %get-tuple-element.127, f32[1024]{0:T(1024)S(1)} %add_rsqrt_fusion.2, ...), kind=kOutput, calls=%fused_computation.160 | convolution fusion | flops 4845985792 | bytes 23641088 | tf_op jit(solution)/shard_map/rf,df->rd/dot_general | solution.py:219
  431.6 21.7 %multiply_reduce_fusion.1 = (f32[12,512]{1,0:T(8,128)S(1)}, f32[12,512,1024]{2,1,0:T(8,128)}) fusion(f32[12,512]{1,0:T(8,128)S(1)} %copy-done.71, f32[12,512,1024]{2,1,0:T(8,128)} %get-tuple-element.121, pred[512,1024]{1,0:T(8,128)(4,1)S(1)} %copy-done.27, bf16[512,12,64]{0,2,1:T(8,128)(2,1)S(1)} %bitcast.146, bf16[1024,12,64]{0,2,1:T(8,128)(2,1)S(1)} %bitcast.130), kind=kOutput, calls=%fused_computation.4 | convolution fusion | flops 836757504 | bytes 53264384 | tf_op jit(solution)/shard_map/qhd,khd->hqk/dot_general | solution.py:79
  453.3 17.4 %multiply_convert_fusion.1 = bf16[12,512,1024]{2,1,0:T(8,128)(2,1)S(1)} fusion(f32[12,512,1024]{2,1,0:T(8,128)} %get-tuple-element.137, f32[12,512]{1,0:T(8,128)S(1)} %get-tuple-element.136, f32[12,512]{1,0:T(8,128)S(1)} %copy-done.71, f32[12,512,1024]{2,1,0:T(8,128)} %get-tuple-element.121, pred[512,1024]{1,0:T(8,128)(4,1)} %get-tuple-element.114), kind=kLoop, calls=%fused_computation.3 | loop fusion | flops 37748736 | bytes 63488000 | tf_op jit(solution)/shard_map/convert_element_type | solution.py:83
  482.2 13.2 %fusion.24 = f32[12,64,1024]{2,1,0:T(8,128)} fusion(bf16[512,12,64]{0,2,1:T(8,128)(2,1)S(1)} %bitcast.150, f32[12,512]{1,0:T(8,128)S(1)} %copy-done.74, f32[12,512,1024]{2,1,0:T(8,128)} %get-tuple-element.119, pred[512,1024]{1,0:T(8,128)(4,1)S(1)} %copy-done.30), kind=kOutput, calls=%fused_computation.52 | convolution fusion | flops 830472192 | bytes 29646848 | tf_op jit(solution)/shard_map/hqk,qhd->khd/dot_general | solution.py:95
  495.4 21.8 %multiply_reduce_fusion = (f32[12,512]{1,0:T(8,128)S(1)}, f32[12,512,1024]{2,1,0:T(8,128)}) fusion(f32[12,512]{1,0:T(8,128)S(1)} %copy-done.74, f32[12,512,1024]{2,1,0:T(8,128)} %get-tuple-element.119, pred[512,1024]{1,0:T(8,128)(4,1)S(1)} %copy-done.31, bf16[512,12,64]{0,2,1:T(8,128)(2,1)S(1)} %bitcast.151, bf16[1024,12,64]{0,2,1:T(8,128)(2,1)S(1)} %bitcast.131), kind=kOutput, calls=%fused_computation.1 | convolution fusion | flops 836757504 | bytes 53264384 | tf_op jit(solution)/shard_map/qhd,khd->hqk/dot_general | solution.py:79
  525.0 21.6 %multiply_reduce_fusion.3 = (f32[12,512]{1,0:T(8,128)S(1)}, f32[12,512,1024]{2,1,0:T(8,128)}) fusion(f32[12,512]{1,0:T(8,128)S(1)} %copy-done.75, f32[12,512,1024]{2,1,0:T(8,128)} %get-tuple-element.125, pred[512,1024]{1,0:T(8,128)(4,1)S(1)} %copy-done.33, bf16[512,12,64]{0,2,1:T(8,128)(2,1)S(1)} %bitcast.148, bf16[1024,12,64]{0,2,1:T(8,128)(2,1)S(1)} %bitcast.127), kind=kOutput, calls=%fused_computation.10 | convolution fusion | flops 836757504 | bytes 53264384 | tf_op jit(solution)/shard_map/qhd,khd->hqk/dot_general | solution.py:79
  546.6 17.2 %multiply_convert_fusion.3 = bf16[12,512,1024]{2,1,0:T(8,128)(2,1)S(1)} fusion(f32[12,512,1024]{2,1,0:T(8,128)} %get-tuple-element.133, f32[12,512]{1,0:T(8,128)S(1)} %get-tuple-element.132, f32[12,512]{1,0:T(8,128)S(1)} %copy-done.75, f32[12,512,1024]{2,1,0:T(8,128)} %get-tuple-element.125, pred[512,1024]{1,0:T(8,128)(4,1)} %get-tuple-element.152), kind=kLoop, calls=%fused_computation.9 | loop fusion | flops 37748736 | bytes 63488000 | tf_op jit(solution)/shard_map/convert_element_type | solution.py:83
  575.3 13.3 %fusion.28 = f32[12,64,1024]{2,1,0:T(8,128)} fusion(bf16[512,12,64]{0,2,1:T(8,128)(2,1)S(1)} %bitcast.153, f32[12,512]{1,0:T(8,128)S(1)} %copy-done.73, f32[12,512,1024]{2,1,0:T(8,128)} %get-tuple-element.123, pred[512,1024]{1,0:T(8,128)(4,1)S(1)} %copy-done.28), kind=kOutput, calls=%fused_computation.54 | convolution fusion | flops 830472192 | bytes 29646848 | tf_op jit(solution)/shard_map/hqk,qhd->khd/dot_general | solution.py:95
  588.5 18.4 %multiply_reduce_fusion.2 = (f32[12,512]{1,0:T(8,128)S(1)}, f32[12,512,1024]{2,1,0:T(8,128)}) fusion(f32[12,512]{1,0:T(8,128)S(1)} %copy-done.73, f32[12,512,1024]{2,1,0:T(8,128)} %get-tuple-element.123, pred[512,1024]{1,0:T(8,128)(4,1)} %get-tuple-element.151, bf16[512,12,64]{0,2,1:T(8,128)(2,1)} %bitcast.152, bf16[1024,12,64]{0,2,1:T(8,128)(2,1)} %bitcast.124), kind=kOutput, calls=%fused_computation.7 | convolution fusion | flops 836757504 | bytes 53264384 | tf_op jit(solution)/shard_map/qhd,khd->hqk/dot_general | solution.py:79
  611.9 15.1 %convert_reduce_fusion.5 = (f32[12,64]{1,0:T(8,128)S(1)}, bf16[12,64,1024]{2,1,0:T(8,128)(2,1)}) fusion(f32[12,64,1024]{2,1,0:T(8,128)} %fusion.28, bf16[512,12,64]{0,2,1:T(8,128)(2,1)} %bitcast.149, f32[12,512]{1,0:T(8,128)S(1)} %copy-done.75, f32[12,512,1024]{2,1,0:T(8,128)} %get-tuple-element.125, pred[512,1024]{1,0:T(8,128)(4,1)} %get-tuple-element.152), kind=kOutput, calls=%fused_computation.162 | convolution fusion | flops 833617152 | bytes 31222784 | tf_op jit(solution)/shard_map/hqk,qhd->khd/dot_general | solution.py:95
  627.0 17.6 %multiply_convert_fusion = bf16[12,512,1024]{2,1,0:T(8,128)(2,1)S(1)} fusion(f32[12,512,1024]{2,1,0:T(8,128)} %get-tuple-element.139, f32[12,512]{1,0:T(8,128)S(1)} %get-tuple-element.138, f32[12,512]{1,0:T(8,128)S(1)} %copy-done.74, f32[12,512,1024]{2,1,0:T(8,128)} %get-tuple-element.119, pred[512,1024]{1,0:T(8,128)(4,1)} %get-tuple-element.115), kind=kLoop, calls=%fused_computation | loop fusion | flops 37748736 | bytes 63488000 | tf_op jit(solution)/shard_map/convert_element_type | solution.py:83
  650.9 22.7 %multiply_convert_fusion.2 = bf16[12,512,1024]{2,1,0:T(8,128)(2,1)} fusion(f32[12,512,1024]{2,1,0:T(8,128)} %get-tuple-element.135, f32[12,512]{1,0:T(8,128)S(1)} %get-tuple-element.134, f32[12,512]{1,0:T(8,128)S(1)} %copy-done.73, f32[12,512,1024]{2,1,0:T(8,128)} %get-tuple-element.123, pred[512,1024]{1,0:T(8,128)(4,1)} %get-tuple-element.151), kind=kLoop, calls=%fused_computation.6 | loop fusion | flops 37748736 | bytes 63488000 | tf_op jit(solution)/shard_map/convert_element_type | solution.py:83
  673.6 9.9 multiply_bitcast_fusion.2
  683.5 8.1 multiply_convert_fusion.5
  695.7 7.2 fusion.102
  706.5 13.3 %convert_reduce_fusion.4 = (f32[12,64]{1,0:T(8,128)S(1)}, bf16[12,64,1024]{2,1,0:T(8,128)(2,1)S(1)}) fusion(f32[12,64,1024]{2,1,0:T(8,128)} %fusion.24, bf16[512,12,64]{0,2,1:T(8,128)(2,1)} %bitcast.147, f32[12,512]{1,0:T(8,128)S(1)} %copy-done.72, f32[12,512,1024]{2,1,0:T(8,128)} %get-tuple-element.121, pred[512,1024]{1,0:T(8,128)(4,1)} %get-tuple-element.114), kind=kOutput, calls=%fused_computation.161 | convolution fusion | flops 833617152 | bytes 31222784 | tf_op jit(solution)/shard_map/hqk,qhd->khd/dot_general | solution.py:95
  721.0 10.3 convolution_add_fusion
  733.1 8.6 fusion.97
  741.8 11.6 %convolution_add_fusion.2 = f32[768,3072]{1,0:T(8,128)} fusion(f32[768,3072]{1,0:T(8,128)S(1)} %fusion.97, bf16[1024,3072]{1,0:T(8,128)(2,1)} %copy-done.40, f32[1024,768]{1,0:T(8,128)S(1)} %copy-done.16, f32[1024]{0:T(1024)S(1)} %copy-done.82, f32[1024]{0:T(1024)S(1)} %copy-done.70, f32[768]{0:T(1024)S(1)} %copy-done.65, f32[768]{0:T(1024)S(1)} %copy-done.63), kind=kOutput, calls=%fused_computation.100 | convolution fusion | flops 4838129664 | bytes 28325888 | tf_op jit(solution)/shard_map/rd,rf->df/dot_general | solution.py:216
  753.5 7.9 fusion.118
  761.4 10.5 convolution_add_fusion.1
  773.8 7.3 fusion.101
  781.1 8.1 fusion.86
  789.2 58.9 %all-reduce.18 = (bf16[768]{0:T(1024)(128)(2,1)S(1)}, bf16[768]{0:T(1024)(128)(2,1)S(1)}, bf16[768]{0:T(1024)(128)(2,1)S(1)}, bf16[768]{0:T(1024)(128)(2,1)S(1)}...) all-reduce(f32[768]{0:T(1024)S(1)} %add.387, ...), channel_id=15, replica_groups=mesh['dp'=2,'fsdp'=16] {'fsdp'}, use_global_device_ids=true, to_apply=%region_29.30.clone | all-reduce | flops 9216 | bytes 55296
  858.5 8.7 add_convert_fusion.4
  867.1 8.6 add_convert_fusion.2
  881.2 52.8 %reduce-scatter.9.cloned.1.call-done = f32[48,3072]{1,0:T(8,128)} async-done(((f32[768,3072]{1,0:T(8,128)}), f32[48,3072]{1,0:T(8,128)}) %reduce-scatter.9.cloned.1.call-update) | async-done | bytes 589840 | tf_op jit(solution)/shard_map/reduce_scatter | solution.py:355
  935.7 114.0 %reduce-scatter.11.cloned.1.call-done = f32[192,768]{1,0:T(8,128)} async-done(((f32[3072,768]{1,0:T(8,128)}), f32[192,768]{1,0:T(8,128)}) %reduce-scatter.11.cloned.1.call-update) | async-done | bytes 589840 | tf_op jit(solution)/shard_map/reduce_scatter | solution.py:357
  1059.4 30.7 %all-reduce.24.cloned.1.call-done = (bf16[48,2304]{1,0:T(8,128)(2,1)}, bf16[48,768]{1,0:T(8,128)(2,1)}, bf16[48,3072]{1,0:T(8,128)(2,1)}, bf16[192,768]{1,0:T(8,128)(2,1)}) async-done(((bf16[48,2304]{1,0:T(8,128)(2,1)}, bf16[48,768]{1,0:T(8,128)(2,1)}, bf16[48,3072]{1,0:T(8,128)(2,1)}, bf16[192,768]{1,0:T(8,128)(2,1)}), (bf16[48,2304]{1,0:T(8,128)(2,1)}, bf16[48,768]{1,0:T(8,128)(2,1)}, ...) | async-done | bytes 884752 | tf_op jit(solution)/shard_map/psum | solution.py:365
  (395 shorter events, 186.1 us)
Async XLA Ops:
  7.2 82.3 %copy-start.8 = (bf16[2048,768]{1,0:T(8,128)(2,1)S(1)}, bf16[2048,768]{1,0:T(8,128)(2,1)}, u32[]{:S(2)}) copy-start(bf16[2048,768]{1,0:T(8,128)(2,1)} %param.16) | copy-start | bytes 9437188
  7.2 86.4 %all-gather.5.cloned.1.call-start = ((), (), s32[]{:S(2)}) async-start(), calls=%async_computation.4 | async-start | bytes 3760128 | tf_op jit(solution)/shard_map/all_gather | solution.py:311
  7.9 285.6 %all-gather.7.cloned.1.call-start = ((), (), s32[]{:S(2)}) async-start(), calls=%async_computation.5 | async-start | bytes 1253376 | tf_op jit(solution)/shard_map/all_gather | solution.py:314
  8.7 295.9 %all-gather.9.cloned.1.call-start = ((), (), s32[]{:S(2)}) async-start(), calls=%async_computation.6 | async-start | bytes 5013504 | tf_op jit(solution)/shard_map/all_gather | solution.py:318
  9.4 306.1 %all-gather.11.cloned.1.call-start = ((), (), s32[]{:S(2)}) async-start(), calls=%async_computation.7 | async-start | bytes 5013504 | tf_op jit(solution)/shard_map/all_gather | solution.py:320
  10.0 867.7 %reduce-scatter.7.cloned.1.call-start = ((), (), s32[]{:S(2)}) async-start(), calls=%async_computation.9 | async-start | bytes 2506752 | tf_op jit(solution)/shard_map/reduce_scatter | solution.py:351
  85.2 19.1 %copy-start.106 = (f32[768]{0:T(1024)}, f32[768]{0:T(1024)S(1)}, u32[]{:S(2)}) copy-start(f32[768]{0:T(1024)S(1)} %convert_element_type.312) | copy-start | bytes 9220
  85.2 19.1 %copy-start.93 = (f32[768]{0:T(1024)}, f32[768]{0:T(1024)S(1)}, u32[]{:S(2)}) copy-start(f32[768]{0:T(1024)S(1)} %convert_element_type.311) | copy-start | bytes 9220
  89.4 14.9 %copy-start.87 = (f32[1024]{0:T(1024)}, f32[1024]{0:T(1024)S(1)}, u32[]{:S(2)}) copy-start(f32[1024]{0:T(1024)S(1)} %get-tuple-element.150) | copy-start | bytes 12292
  90.8 13.5 %copy-start.95 = (f32[1024]{0:T(1024)}, f32[1024]{0:T(1024)S(1)}, u32[]{:S(2)}) copy-start(f32[1024]{0:T(1024)S(1)} %add_rsqrt_fusion.3) | copy-start | bytes 12292
  104.3 151.6 %copy-start.5 = (bf16[1024,768]{0,1:T(8,128)(2,1)}, bf16[1024,768]{0,1:T(8,128)(2,1)S(1)}, u32[]{:S(2)}) copy-start(bf16[1024,768]{0,1:T(8,128)(2,1)S(1)} %copy.69) | copy-start | bytes 4718596
  118.2 64.6 %copy-start.4 = (bf16[1024,768]{0,1:T(8,128)(2,1)}, bf16[1024,768]{0,1:T(8,128)(2,1)S(1)}, u32[]{:S(2)}) copy-start(bf16[1024,768]{0,1:T(8,128)(2,1)S(1)} %copy.65) | copy-start | bytes 4718596
  144.8 24.9 %copy-start.21 = (bf16[1024,768]{0,1:T(8,128)(2,1)S(1)}, bf16[1024,768]{0,1:T(8,128)(2,1)}, u32[]{:S(2)}) copy-start(bf16[1024,768]{0,1:T(8,128)(2,1)} %copy.63) | copy-start | bytes 4718596
  157.1 12.6 %copy-start.76 = (f32[12,512]{1,0:T(8,128)}, f32[12,512]{1,0:T(8,128)S(1)}, u32[]{:S(2)}) copy-start(f32[12,512]{1,0:T(8,128)S(1)} %get-tuple-element.122) | copy-start | bytes 73732
  157.1 16.2 %copy-start.1 = (f32[12,512,1024]{2,1,0:T(8,128)S(1)}, f32[12,512,1024]{2,1,0:T(8,128)}, u32[]{:S(2)}) copy-start(f32[12,512,1024]{2,1,0:T(8,128)} %get-tuple-element.123) | copy-start | bytes 75497472
  169.7 13.1 %copy-start.83 = (f32[12,512]{1,0:T(8,128)}, f32[12,512]{1,0:T(8,128)S(1)}, u32[]{:S(2)}) copy-start(f32[12,512]{1,0:T(8,128)S(1)} %fusion.1) | copy-start | bytes 73732
  194.9 16.3 %copy-start.3 = (f32[12,512,1024]{2,1,0:T(8,128)S(1)}, f32[12,512,1024]{2,1,0:T(8,128)}, u32[]{:S(2)}) copy-start(f32[12,512,1024]{2,1,0:T(8,128)} %get-tuple-element.125) | copy-start | bytes 75497472
  194.9 16.4 %copy-start.32 = (pred[512,1024]{1,0:T(8,128)(4,1)S(1)}, pred[512,1024]{1,0:T(8,128)(4,1)}, u32[]{:S(2)}) copy-start(pred[512,1024]{1,0:T(8,128)(4,1)} %get-tuple-element.152) | copy-start | bytes 1572868
  219.7 24.6 %copy-start.23 = (bf16[1024,768]{0,1:T(8,128)(2,1)S(1)}, bf16[1024,768]{0,1:T(8,128)(2,1)}, u32[]{:S(2)}) copy-start(bf16[1024,768]{0,1:T(8,128)(2,1)} %copy.67) | copy-start | bytes 4718596
  232.1 15.4 %copy-start.2 = (f32[12,512,1024]{2,1,0:T(8,128)S(1)}, f32[12,512,1024]{2,1,0:T(8,128)}, u32[]{:S(2)}) copy-start(f32[12,512,1024]{2,1,0:T(8,128)} %get-tuple-element.119) | copy-start | bytes 75497472
  255.9 24.4 %copy-start.60 = (bf16[512,12,64]{0,2,1:T(8,128)(2,1)S(1)}, bf16[512,12,64]{0,2,1:T(8,128)(2,1)}, u32[]{:S(2)}) copy-start(bf16[512,12,64]{0,2,1:T(8,128)(2,1)} %fusion.113) | copy-start | bytes 2359300
  268.0 16.1 %copy-start = (f32[12,512,1024]{2,1,0:T(8,128)S(1)}, f32[12,512,1024]{2,1,0:T(8,128)}, u32[]{:S(2)}) copy-start(f32[12,512,1024]{2,1,0:T(8,128)} %get-tuple-element.121) | copy-start | bytes 75497472
  297.5 124.8 %copy-start.6 = (f32[1024,768]{1,0:T(8,128)}, f32[1024,768]{1,0:T(8,128)S(1)}, u32[]{:S(2)}) copy-start(f32[1024,768]{1,0:T(8,128)S(1)} %get-tuple-element.127) | copy-start | bytes 9437188
  297.6 124.8 %copy-start.66 = (f32[1024]{0:T(1024)}, f32[1024]{0:T(1024)S(1)}, u32[]{:S(2)}) copy-start(f32[1024]{0:T(1024)S(1)} %broadcast_multiply_fusion.10) | copy-start | bytes 12292
  298.1 124.3 %copy-start.78 = (f32[1024]{0:T(1024)}, f32[1024]{0:T(1024)S(1)}, u32[]{:S(2)}) copy-start(f32[1024]{0:T(1024)S(1)} %add_rsqrt_fusion.2) | copy-start | bytes 12292
  299.8 15.7 %copy-start.68 = (f32[1024]{0:T(1024)}, f32[1024]{0:T(1024)S(1)}, u32[]{:S(2)}) copy-start(f32[1024]{0:T(1024)S(1)} %broadcast_multiply_fusion.8) | copy-start | bytes 12292
  302.0 13.5 %copy-start.80 = (f32[1024]{0:T(1024)}, f32[1024]{0:T(1024)S(1)}, u32[]{:S(2)}) copy-start(f32[1024]{0:T(1024)S(1)} %add_rsqrt_fusion) | copy-start | bytes 12292
  315.6 13.5 %copy-start.110 = (bf16[768,3072]{1,0:T(8,128)(2,1)S(1)}, bf16[768,3072]{1,0:T(8,128)(2,1)}, u32[]{:S(2)}) copy-start(bf16[768,3072]{1,0:T(8,128)(2,1)} %all-gather.9.cloned.1.call-done) | copy-start | bytes 14155780
  315.6 20.2 %slice-start = ((s8[12582912]{0:T(1024)(128)(4,1)}), s8[4194304]{0:T(1024)(128)(4,1)S(1)}, s32[]{:S(2)}) async-start(s8[12582912]{0:T(1024)(128)(4,1)} %bitcast.164), calls=%async_computation.13 | async-start | bytes 8388608
  315.6 20.2 %slice-start.1 = ((s8[12582912]{0:T(1024)(128)(4,1)}), s8[4194304]{0:T(1024)(128)(4,1)S(1)}, s32[]{:S(2)}) async-start(s8[12582912]{0:T(1024)(128)(4,1)} %bitcast.164), calls=%async_computation.14 | async-start | bytes 8388608
  335.8 61.6 %copy-start.48 = (bf16[2048,768]{1,0:T(8,128)(2,1)S(1)}, bf16[2048,768]{1,0:T(8,128)(2,1)}, u32[]{:S(2)}) copy-start(bf16[2048,768]{1,0:T(8,128)(2,1)} %param.17) | copy-start | bytes 9437188
  409.4 12.9 %copy-start.36 = (bf16[1024,3072]{1,0:T(8,128)(2,1)}, bf16[1024,3072]{1,0:T(8,128)(2,1)S(1)}, u32[]{:S(2)}) copy-start(bf16[1024,3072]{1,0:T(8,128)(2,1)S(1)} %get-tuple-element.146) | copy-start | bytes 18874372
  431.6 21.7 %copy-start.52 = (bf16[512,768]{0,1:T(8,128)(2,1)}, bf16[512,768]{0,1:T(8,128)(2,1)S(1)}, u32[]{:S(2)}) copy-start(bf16[512,768]{0,1:T(8,128)(2,1)S(1)} %get-tuple-element.92) | copy-start | bytes 2359300
  482.1 13.3 %copy-start.25 = (bf16[1024,768]{0,1:T(8,128)(2,1)S(1)}, bf16[1024,768]{0,1:T(8,128)(2,1)}, u32[]{:S(2)}) copy-start(bf16[1024,768]{0,1:T(8,128)(2,1)} %copy.67) | copy-start | bytes 4718596
  482.1 13.2 %copy-start.31 = (pred[512,1024]{1,0:T(8,128)(4,1)S(1)}, pred[512,1024]{1,0:T(8,128)(4,1)}, u32[]{:S(2)}) copy-start(pred[512,1024]{1,0:T(8,128)(4,1)} %get-tuple-element.115) | copy-start | bytes 1572868
  482.1 13.2 %copy-start.55 = (bf16[512,768]{0,1:T(8,128)(2,1)S(1)}, bf16[512,768]{0,1:T(8,128)(2,1)}, u32[]{:S(2)}) copy-start(bf16[512,768]{0,1:T(8,128)(2,1)} %get-tuple-element.93) | copy-start | bytes 2359300
  525.0 21.6 %copy-start.53 = (bf16[512,768]{0,1:T(8,128)(2,1)}, bf16[512,768]{0,1:T(8,128)(2,1)S(1)}, u32[]{:S(2)}) copy-start(bf16[512,768]{0,1:T(8,128)(2,1)S(1)} %get-tuple-element.90) | copy-start | bytes 2359300
  588.5 18.4 %copy-start.19 = (f32[1024,768]{1,0:T(8,128)S(1)}, f32[1024,768]{1,0:T(8,128)}, u32[]{:S(2)}) copy-start(f32[1024,768]{1,0:T(8,128)} %copy-done.18) | copy-start | bytes 9437188
  611.9 267.6 %reduce-scatter.5.cloned.1.call-start = ((), (), s32[]{:S(2)}) async-start(), calls=%async_computation.8 | async-start | bytes 7520256 | tf_op jit(solution)/shard_map/reduce_scatter | solution.py:348
  706.5 14.5 %copy-start.11 = (bf16[2048,768]{1,0:T(8,128)(2,1)S(1)}, bf16[2048,768]{1,0:T(8,128)(2,1)}, u32[]{:S(2)}) copy-start(bf16[2048,768]{1,0:T(8,128)(2,1)} %param.16) | copy-start | bytes 9437188
  706.5 14.5 %copy-start.43 = (bf16[12,64,1024]{2,1,0:T(8,128)(2,1)S(1)}, bf16[12,64,1024]{2,1,0:T(8,128)(2,1)}, u32[]{:S(2)}) copy-start(bf16[12,64,1024]{2,1,0:T(8,128)(2,1)} %multiply_convert_fusion.4) | copy-start | bytes 4718596
  706.5 14.5 %copy-start.59 = (bf16[1024,12,64]{0,2,1:T(8,128)(2,1)S(1)}, bf16[1024,12,64]{0,2,1:T(8,128)(2,1)}, u32[]{:S(2)}) copy-start(bf16[1024,12,64]{0,2,1:T(8,128)(2,1)} %get-tuple-element.75) | copy-start | bytes 4718596
  706.5 14.5 %copy-start.86 = (f32[1024]{0:T(1024)S(1)}, f32[1024]{0:T(1024)}, u32[]{:S(2)}) copy-start(f32[1024]{0:T(1024)} %copy-done.85) | copy-start | bytes 12292
  706.5 14.5 %copy-start.98 = (f32[1024]{0:T(1024)S(1)}, f32[1024]{0:T(1024)}, u32[]{:S(2)}) copy-start(f32[1024]{0:T(1024)} %copy-done.97) | copy-start | bytes 12292
  731.3 202.6 %reduce-scatter.9.cloned.1.call-start = ((), (), s32[]{:S(2)}) async-start(), calls=%async_computation.10 | async-start | bytes 10027008 | tf_op jit(solution)/shard_map/reduce_scatter | solution.py:355
  753.5 296.2 %reduce-scatter.11.cloned.1.call-start = ((), (), s32[]{:S(2)}) async-start(), calls=%async_computation.11 | async-start | bytes 10027008 | tf_op jit(solution)/shard_map/reduce_scatter | solution.py:357
  772.1 318.1 %all-reduce.24.cloned.1.call-start = ((), (), s32[]{:S(2)}) async-start(), calls=%async_computation.12 | async-start | bytes 1769472 | tf_op jit(solution)/shard_map/psum | solution.py:365
  875.8 175.8 %copy-start.13 = (bf16[2048,768]{1,0:T(8,128)(2,1)S(1)}, bf16[2048,768]{1,0:T(8,128)(2,1)}, u32[]{:S(2)}) copy-start(bf16[2048,768]{1,0:T(8,128)(2,1)} %param.16) | copy-start | bytes 9437188
  (82 other events, 450.9 us)
Sparse Core Ops, SparseCore 0:
  10.3 49.9 all-gather.4
  62.6 37.2 all-gather.6
  102.2 52.1 all-gather.8
  156.5 51.7 all-gather.10
  612.0 60.1 reduce-scatter.6
  731.4 87.4 reduce-scatter.4
  823.0 110.8 reduce-scatter.8
  938.6 111.0 reduce-scatter.10
  1053.3 36.7 all-reduce.23
where the time goes:
time: 1120 us; the launch traced here: 1100 us
  matrix products  511 us (46%)
  waiting for transfers between devices  200 us (18%)
  other arithmetic  186 us (17%)
  blocking collectives  127 us (11%)
  local copies, waits for them, and re-layouts  60.9 us (5%)
  between operations  18.3 us (2%)
    unnamed x2, blocking collectives  122 us
    reduce_scatter x1, waiting for transfers between devices, on_device(): lax.psum_scatter(p11, 'fsdp', scatter_dimension=0, tiled=True)  114 us
    dot_general x4, matrix products, attend_backward(): jnp.einsum('qhd,khd->hqk', grad_block, value, preferred_element_type=jnp....  83.5 us
    convert_element_type x4, other arithmetic, attend_backward(): grad_scores = (soft * (grad_soft - center)).astype(jnp.bfloat16)  74.9 us
    dot_general x2, matrix products, layer_forward(): jnp.dot(second_in, up_weight, preferred_element_type=jnp.float32)  72.5 us
    dot_general x4, matrix products, attend_backward(): jnp.einsum('hqk,qhd->khd', soft.astype(jnp.bfloat16), grad_block, preferr...  54.9 us
    reduce_scatter x1, waiting for transfers between devices, on_device(): lax.psum_scatter(p9, 'fsdp', scatter_dimension=0, tiled=True)  52.8 us
    reduce_sum x4, other arithmetic, attend_forward(): total = jnp.sum(exponent, axis=-1, keepdims=True)  50.7 us
  transfers between devices with their start and end apart: 9, of which 3 were waited for; matrix products, arithmetic and copies ran while one was open for 39% of the time, Pallas kernels for 0%

commit v1 on v0

v1 whole, which is shorter than its diff:
```python
import functools

import jax
import jax.numpy as jnp
from jax import lax
from jax.experimental import pallas as pl
from jax.experimental.pallas import tpu as pltpu
from jax.sharding import PartitionSpec as P

H = 12
HD = 64
ROWS = 1024
EPS = 1e-06
F32 = jnp.float32
BF16 = jnp.bfloat16
VMEM_LIMIT = 60 * 1024 * 1024

ROOT_HALF = 0.7071067811865476
ROOT_INV_TWO_PI = 0.3989422804014327

NN = (((1,), (0,)), ((), ()))
NT = (((1,), (1,)), ((), ()))


def mm(a, b, dims=NN):
    return lax.dot_general(a, b, dims, preferred_element_type=F32)


def params(**kw):
    return pltpu.CompilerParams(vmem_limit_bytes=VMEM_LIMIT, **kw)


def norm_stats(x):
    mean = jnp.mean(x, axis=-1, keepdims=True)
    cen = x - mean
    var = jnp.mean(cen * cen, axis=-1, keepdims=True)
    inv = lax.rsqrt(var + EPS)
    return cen * inv, inv


def proj_body(x_ref, gain_ref, shift_ref, w_ref, bias_ref, scale_ref, qkv_ref):
    n, _ = norm_stats(x_ref[...].astype(F32))
    h = (n * gain_ref[...] + shift_ref[...]).astype(BF16)
    p = mm(h, w_ref[...])
    qkv_ref[...] = ((p + bias_ref[...]) * scale_ref[...]).astype(BF16)


def project(x, gain, shift, w, bias, scale):
    rows, d = x.shape
    cols = w.shape[1]
    tile = 512
    row = pl.BlockSpec((1, d), lambda i: (0, 0))
    wide = pl.BlockSpec((1, cols), lambda i: (0, 0))
    return pl.pallas_call(
        proj_body,
        grid=(rows // tile,),
        in_specs=[
            pl.BlockSpec((tile, d), lambda i: (i, 0)),
            row,
            row,
            pl.BlockSpec((d, cols), lambda i: (0, 0)),
            wide,
            wide,
        ],
        out_specs=pl.BlockSpec((tile, cols), lambda i: (i, 0)),
        out_shape=jax.ShapeDtypeStruct((rows, cols), BF16),
        compiler_params=params(),
        name="project",
        cost_estimate=pl.CostEstimate(
            flops=2 * rows * d * cols, bytes_accessed=2 * rows * (d + cols), transcendentals=0
        ),
    )(x, gain, shift, w, bias, scale)


QT = 256


def half_mask(value, hh):
    lane = lax.broadcasted_iota(jnp.int32, value.shape, 1)
    keep = lane < HD if hh == 0 else lane >= HD
    return jnp.where(keep, value, jnp.zeros_like(value))


def attend_body(q_ref, k_ref, v_ref, segc_ref, segr_ref, o_ref, p_ref, bias_ref):
    rows = q_ref.shape[0]

    @pl.when(pl.program_id(1) == 0)
    def _():
        bias_ref[...] = jnp.where(segc_ref[...] == segr_ref[...], 0.0, -1e30)

    k = k_ref[...]
    v = v_ref[...]
    for t in range(rows // QT):
        sl = pl.ds(t * QT, QT)
        out = None
        for hh in range(2):
            q = half_mask(q_ref[sl, :], hh)
            s = mm(q, k, NT) + bias_ref[sl, :]
            peak = jnp.max(s, axis=-1, keepdims=True)
            e = jnp.exp(s - peak)
            total = jnp.sum(e, axis=-1, keepdims=True)
            p = (e * (1.0 / total)).astype(BF16)
            p_ref[hh, sl, :] = p
            o = mm(p, v)
            if hh == 0:
                out = o
            else:
                lane = lax.broadcasted_iota(jnp.int32, o.shape, 1)
                out = jnp.where(lane < HD, out, o)
        o_ref[sl, :] = out.astype(BF16)


def attend(qkv, segc, segr):
    rows = qkv.shape[0]
    d = qkv.shape[1] // 3
    mb = rows // ROWS
    pairs = d // 128
    return pl.pallas_call(
        attend_body,
        grid=(mb, pairs),
        in_specs=[
            pl.BlockSpec((ROWS, 128), lambda m, h: (m, h)),
            pl.BlockSpec((ROWS, 128), lambda m, h: (m, pairs + h)),
            pl.BlockSpec((ROWS, 128), lambda m, h: (m, 2 * pairs + h)),
            pl.BlockSpec((ROWS, 1), lambda m, h: (m, 0)),
            pl.BlockSpec((None, 1, ROWS), lambda m, h: (m, 0, 0)),
        ],
        out_specs=[
            pl.BlockSpec((ROWS, 128), lambda m, h: (m, h)),
            pl.BlockSpec((None, 2, ROWS, ROWS), lambda m, h: (m, h, 0, 0)),
        ],
        out_shape=[
            jax.ShapeDtypeStruct((rows, d), BF16),
            jax.ShapeDtypeStruct((mb, 2 * pairs, ROWS, ROWS), BF16),
        ],
        scratch_shapes=[pltpu.VMEM((ROWS, ROWS), F32)],
        compiler_params=params(),
        name="attend",
        cost_estimate=pl.CostEstimate(
            flops=mb * pairs * 2 * 4 * ROWS * ROWS * 256,
            bytes_accessed=mb * pairs * 2 * ROWS * ROWS * 2,
            transcendentals=mb * pairs * 2 * ROWS * ROWS,
        ),
    )(qkv, qkv, qkv, segc, segr)


def attend_back_body(q_ref, k_ref, v_ref, p_ref, o_ref, g_ref, dq_ref, dk_ref, dv_ref, ds_ref):
    rows = q_ref.shape[0]
    k = k_ref[...]
    v = v_ref[...]
    q_t = q_ref[...].T
    g_t = g_ref[...].T
    prod = g_ref[...].astype(F32) * o_ref[...].astype(F32)
    dk_parts = []
    dv_parts = []
    dq_parts = []
    for hh in range(2):
        half = slice(hh * HD, (hh + 1) * HD)
        center = jnp.sum(half_mask(prod, hh), axis=-1, keepdims=True)
        for t in range(rows // QT):
            sl = pl.ds(t * QT, QT)
            ts = slice(t * QT, (t + 1) * QT)
            d_soft = mm(half_mask(g_ref[sl, :], hh), v, NT)
            ds = p_ref[hh, sl, :].astype(F32) * (d_soft - center[ts, :])
            ds_ref[hh, sl, :] = ds.astype(BF16)
        dv_parts.append(mm(g_t[half, :], p_ref[hh]))
        dk_parts.append(mm(q_t[half, :], ds_ref[hh]))
        dq_parts.append(mm(ds_ref[hh], k))
    lane = lax.broadcasted_iota(jnp.int32, dq_parts[0].shape, 1)
    dq_ref[...] = (jnp.where(lane < HD, dq_parts[0], dq_parts[1]) * 0.125).astype(BF16)
    dk_ref[...] = jnp.concatenate(dk_parts, axis=0).T.astype(BF16)
    dv_ref[...] = jnp.concatenate(dv_parts, axis=0).T.astype(BF16)


def attend_back(qkv, soft, mixed, d_mixed):
    rows = qkv.shape[0]
    d = qkv.shape[1] // 3
    mb = rows // ROWS
    pairs = d // 128
    blk = pl.BlockSpec((ROWS, 128), lambda m, h: (m, h))
    shape = jax.ShapeDtypeStruct((rows, d), BF16)
    return pl.pallas_call(
        attend_back_body,
        grid=(mb, pairs),
        in_specs=[
            blk,
            pl.BlockSpec((ROWS, 128), lambda m, h: (m, pairs + h)),
            pl.BlockSpec((ROWS, 128), lambda m, h: (m, 2 * pairs + h)),
            pl.BlockSpec((None, 2, ROWS, ROWS), lambda m, h: (m, h, 0, 0)),
            blk,
            blk,
        ],
        out_specs=[blk, blk, blk],
        out_shape=[shape, shape, shape],
        scratch_shapes=[pltpu.VMEM((2, ROWS, ROWS), BF16)],
        compiler_params=params(),
        name="attend_back",
        cost_estimate=pl.CostEstimate(
            flops=mb * pairs * 2 * 8 * ROWS * ROWS * 256,
            bytes_accessed=mb * pairs * 2 * ROWS * ROWS * 2,
            transcendentals=0,
        ),
    )(qkv, qkv, qkv, soft, mixed, d_mixed)


def out_body(x_ref, m_ref, w_ref, bias_ref, gain_ref, shift_ref, resid_ref, h_ref):
    resid = x_ref[...].astype(F32) + mm(m_ref[...], w_ref[...]) + bias_ref[...]
    resid_ref[...] = resid
    n, _ = norm_stats(resid)
    h_ref[...] = (n * gain_ref[...] + shift_ref[...]).astype(BF16)


def out_project(x, mixed, w, bias, gain, shift):
    rows, d = x.shape
    tile = 512
    blk = pl.BlockSpec((tile, d), lambda i: (i, 0))
    row = pl.BlockSpec((1, d), lambda i: (0, 0))
    return pl.pallas_call(
        out_body,
        grid=(rows // tile,),
        in_specs=[blk, blk, pl.BlockSpec((d, d), lambda i: (0, 0)), row, row, row],
        out_specs=[blk, blk],
        out_shape=[
            jax.ShapeDtypeStruct((rows, d), F32),
            jax.ShapeDtypeStruct((rows, d), BF16),
        ],
        compiler_params=params(),
        name="out_project",
        cost_estimate=pl.CostEstimate(
            flops=2 * rows * d * d, bytes_accessed=rows * d * 10, transcendentals=0
        ),
    )(x, mixed, w, bias, gain, shift)


FC = 512
RT = 512


def gelu_parts(u):
    cdf = 0.5 * (1.0 + lax.erf(u * ROOT_HALF))
    bell = jnp.exp(-0.5 * u * u) * ROOT_INV_TWO_PI
    return u * cdf, cdf + u * bell


def mlp_body(h_ref, ht_ref, g_ref, gt_ref, wu_ref, bu_ref, wd_ref, acc_ref, dh_ref, dwu_ref, dwd_ref, dbu_ref,
             act_ref, du_ref):
    rows = h_ref.shape[0]

    @pl.when(pl.program_id(0) == 0)
    def _():
        acc_ref[...] = jnp.zeros_like(acc_ref)
        dh_ref[...] = jnp.zeros_like(dh_ref)

    wu = wu_ref[...]
    wd = wd_ref[...]
    bias_sum = None
    for t in range(rows // RT):
        sl = pl.ds(t * RT, RT)
        u = mm(h_ref[sl, :], wu) + bu_ref[...]
        act, slope = gelu_parts(u)
        act_ref[sl, :] = act.astype(BF16)
        du = mm(g_ref[sl, :], wd, NT) * slope
        part = jnp.sum(du, axis=0, keepdims=True)
        bias_sum = part if bias_sum is None else bias_sum + part
        du_ref[sl, :] = du.astype(BF16)
        acc_ref[sl, :] += mm(act_ref[sl, :], wd)
        dh_ref[sl, :] += mm(du_ref[sl, :], wu, NT)
    dbu_ref[...] = bias_sum
    dwu_ref[...] = mm(ht_ref[...], du_ref[...]).astype(dwu_ref.dtype)
    dwd_ref[...] = mm(gt_ref[...], act_ref[...]).T.astype(dwd_ref.dtype)


def mlp(h, ht, g, gt, wu, bu, wd):
    rows, d = h.shape
    ff = wu.shape[1]
    one = pl.Buffered(1)
    whole = pl.BlockSpec((rows, d), lambda c: (0, 0), pipeline_mode=one)
    whole_t = pl.BlockSpec((d, rows), lambda c: (0, 0), pipeline_mode=one)
    return pl.pallas_call(
        mlp_body,
        grid=(ff // FC,),
        in_specs=[
            whole,
            whole_t,
            whole,
            whole_t,
            pl.BlockSpec((d, FC), lambda c: (0, c)),
            pl.BlockSpec((1, FC), lambda c: (0, c)),
            pl.BlockSpec((FC, d), lambda c: (c, 0)),
        ],
        out_specs=[
            whole,
            whole,
            pl.BlockSpec((d, FC), lambda c: (0, c)),
            pl.BlockSpec((FC, d), lambda c: (c, 0)),
            pl.BlockSpec((1, FC), lambda c: (0, c)),
        ],
        out_shape=[
            jax.ShapeDtypeStruct((rows, d), F32),
            jax.ShapeDtypeStruct((rows, d), F32),
            jax.ShapeDtypeStruct((d, ff), BF16),
            jax.ShapeDtypeStruct((ff, d), BF16),
            jax.ShapeDtypeStruct((1, ff), F32),
        ],
        scratch_shapes=[pltpu.VMEM((rows, FC), BF16), pltpu.VMEM((rows, FC), BF16)],
        compiler_params=params(),
        name="mlp",
        cost_estimate=pl.CostEstimate(
            flops=12 * rows * d * ff, bytes_accessed=rows * d * 20 + 8 * d * ff, transcendentals=3 * rows * ff
        ),
    )(h, ht, g, gt, wu, bu, wd)


def fold(ref, step, value):
    part = jnp.sum(value, axis=0, keepdims=True)

    @pl.when(step == 0)
    def _():
        ref[...] = part

    @pl.when(step != 0)
    def _():
        ref[...] += part


def norm_pull(grad, n, inv, gain):
    dn = grad * gain
    plain = jnp.mean(dn, axis=-1, keepdims=True)
    cross = jnp.mean(dn * n, axis=-1, keepdims=True)
    return inv * (dn - plain - n * cross)


def mid_body(resid_ref, acc_ref, dh_ref, g_ref, mixed_ref, w_ref, bias_ref, gain_ref,
             y_ref, dr_ref, dm_ref, dw_ref, dgain_ref, dshift_ref, dob_ref, ddb_ref, sum_ref):
    step = pl.program_id(0)
    resid = resid_ref[...]
    y_ref[...] = (resid + acc_ref[...] + bias_ref[...]).astype(BF16)
    g = g_ref[...].astype(F32)
    n, inv = norm_stats(resid)
    dh = dh_ref[...]
    fold(dgain_ref, step, dh * n)
    fold(dshift_ref, step, dh)
    fold(ddb_ref, step, g)
    dr = g + norm_pull(dh, n, inv, gain_ref[...])
    dr_ref[...] = dr
    fold(dob_ref, step, dr)
    low = dr.astype(BF16)
    dm_ref[...] = mm(low, w_ref[...], NT).astype(BF16)
    dw = mm(mixed_ref[...].T, low)

    @pl.when(step == 0)
    def _():
        sum_ref[...] = dw

    @pl.when(step != 0)
    def _():
        sum_ref[...] += dw

    @pl.when(step == pl.num_programs(0) - 1)
    def _():
        dw_ref[...] = sum_ref[...].astype(dw_ref.dtype)


def middle(resid, acc, dh, g, mixed, w, bias, gain):
    rows, d = resid.shape
    tile = 512
    blk = pl.BlockSpec((tile, d), lambda i: (i, 0))
    row = pl.BlockSpec((1, d), lambda i: (0, 0))
    mat = pl.BlockSpec((d, d), lambda i: (0, 0))
    vec = jax.ShapeDtypeStruct((1, d), F32)
    return pl.pallas_call(
        mid_body,
        grid=(rows // tile,),
        in_specs=[blk, blk, blk, blk, blk, mat, row, row],
        out_specs=[blk, blk, blk, mat, row, row, row, row],
        out_shape=[
            jax.ShapeDtypeStruct((rows, d), BF16),
            jax.ShapeDtypeStruct((rows, d), F32),
            jax.ShapeDtypeStruct((rows, d), BF16),
            jax.ShapeDtypeStruct((d, d), BF16),
            vec,
            vec,
            vec,
            vec,
        ],
        scratch_shapes=[pltpu.VMEM((d, d), F32)],
        compiler_params=params(),
        name="middle",
        cost_estimate=pl.CostEstimate(
            flops=4 * rows * d * d, bytes_accessed=rows * d * 24, transcendentals=0
        ),
    )(resid, acc, dh, g, mixed, w, bias, gain)


def last_body(x_ref, dr_ref, dq_ref, dk_ref, dv_ref, w_ref, gain_ref, shift_ref,
              dx_ref, dw_ref, dgain_ref, dshift_ref, dqb_ref, dvb_ref, sum_ref):
    step = pl.program_id(0)
    d = x_ref.shape[1]
    n, inv = norm_stats(x_ref[...].astype(F32))
    h_t = (n * gain_ref[...] + shift_ref[...]).astype(BF16).T
    dh = None
    for j, ref in enumerate((dq_ref, dk_ref, dv_ref)):
        cols = pl.ds(j * d, d)
        part = ref[...]
        term = mm(part, w_ref[:, cols], NT)
        dh = term if dh is None else dh + term
        dw = mm(h_t, part)

        @pl.when(step == 0)
        def _():
            sum_ref[:, cols] = dw

        @pl.when(step != 0)
        def _():
            sum_ref[:, cols] += dw

    fold(dqb_ref, step, dq_ref[...].astype(F32))
    fold(dvb_ref, step, dv_ref[...].astype(F32))
    fold(dgain_ref, step, dh * n)
    fold(dshift_ref, step, dh)
    dx_ref[...] = (dr_ref[...] + norm_pull(dh, n, inv, gain_ref[...])).astype(BF16)

    @pl.when(step == pl.num_programs(0) - 1)
    def _():
        dw_ref[...] = sum_ref[...].astype(dw_ref.dtype)


def last(x, dr, dq, dk, dv, w, gain, shift):
    rows, d = x.shape
    tile = 512
    blk = pl.BlockSpec((tile, d), lambda i: (i, 0))
    row = pl.BlockSpec((1, d), lambda i: (0, 0))
    mat = pl.BlockSpec((d, 3 * d), lambda i: (0, 0))
    vec = jax.ShapeDtypeStruct((1, d), F32)
    return pl.pallas_call(
        last_body,
        grid=(rows // tile,),
        in_specs=[blk, blk, blk, blk, blk, mat, row, row],
        out_specs=[blk, mat, row, row, row, row],
        out_shape=[
            jax.ShapeDtypeStruct((rows, d), BF16),
            jax.ShapeDtypeStruct((d, 3 * d), BF16),
            vec,
            vec,
            vec,
            vec,
        ],
        scratch_shapes=[pltpu.VMEM((d, 3 * d), F32)],
        compiler_params=params(),
        name="last",
        cost_estimate=pl.CostEstimate(
            flops=12 * rows * d * d, bytes_accessed=rows * d * 14, transcendentals=0
        ),
    )(x, dr, dq, dk, dv, w, gain, shift)


def layer(tokens, cotangent, segment_ids, full):
    (
        first_gain,
        first_shift,
        triple_weight,
        query_bias,
        value_bias,
        out_weight,
        out_bias,
        second_gain,
        second_shift,
        up_weight,
        up_bias,
        down_weight,
        down_bias,
    ) = full
    rows, d = tokens.shape
    row = lambda v: v.astype(F32).reshape(1, -1)
    zero = jnp.zeros((d,), BF16)
    bias = row(jnp.concatenate([query_bias, zero, value_bias]))
    scale = jnp.concatenate([jnp.full((1, d), 0.125, F32), jnp.ones((1, 2 * d), F32)], axis=1)
    segc = segment_ids.reshape(rows, 1)
    segr = segment_ids.reshape(rows // ROWS, 1, ROWS)
    qkv = project(tokens, row(first_gain), row(first_shift), triple_weight, bias, scale)
    mixed, soft = attend(qkv, segc, segr)
    resid, h = out_project(tokens, mixed, out_weight, row(out_bias), row(second_gain), row(second_shift))
    acc, dh, dwu, dwd, dbu = mlp(h, h.T, cotangent, cotangent.T, up_weight, row(up_bias), down_weight)
    y, dr, dm, dwo, dg2, ds2, dob, ddb = middle(
        resid, acc, dh, cotangent, mixed, out_weight, row(down_bias), row(second_gain)
    )
    dq, dk, dv = attend_back(qkv, soft, mixed, dm)
    dx, dwt, dg1, ds1, dqb, dvb = last(tokens, dr, dq, dk, dv, triple_weight, row(first_gain), row(first_shift))
    return y, dx, (dg1, ds1, dwt, dqb, dvb, dwo, dob, dg2, ds2, dwu, dbu, dwd, ddb)


def on_device(tokens, cotangent, segment_ids, *shards):
    gather = lambda s: lax.all_gather(s, "fsdp", axis=0, tiled=True)
    vectors = [s for s in shards if s.ndim == 1]
    n = lax.axis_size("fsdp")
    packed = gather(jnp.concatenate(vectors).reshape(1, -1))
    full = []
    at = 0
    for s in shards:
        if s.ndim == 1:
            full.append(packed[:, at : at + s.shape[0]].reshape(-1))
            at += s.shape[0]
        else:
            full.append(gather(s))
    y, dx, parts = layer(tokens, cotangent, segment_ids, full)
    small = jnp.concatenate([p.reshape(n, -1) for p, s in zip(parts, shards) if s.ndim == 1], axis=1)
    small = lax.psum_scatter(small, "fsdp", scatter_dimension=0, tiled=True).reshape(-1)
    small = lax.psum(small, "dp")
    grads = []
    at = 0
    for p, s in zip(parts, shards):
        if s.ndim == 1:
            grads.append(small[at : at + s.shape[0]])
            at += s.shape[0]
        else:
            one = lax.psum_scatter(p, "fsdp", scatter_dimension=0, tiled=True)
            grads.append(lax.psum(one, "dp").astype(F32))
    return (y, dx, *grads)


def solution(mesh):
    tok = P(("dp", "fsdp"), None)
    vec = P("fsdp")
    mat = P("fsdp", None)
    weights = (vec, vec, mat, vec, vec, mat, vec, vec, vec, mat, vec, mat, vec)
    return jax.shard_map(
        on_device,
        mesh=mesh,
        in_specs=(tok, tok, P(("dp", "fsdp")), *weights),
        out_specs=(tok, tok, *weights),
        check_vma=False,
    )
```

time: 1120 us -> 700 us (0.62); the launches traced: 1100 us -> 699 us
  matrix products: 511 us -> 0 us
  Pallas kernels: 0 us -> 272 us
  other arithmetic: 186 us -> 8.47 us
  waiting for transfers between devices: 200 us -> 250 us
  local copies, waits for them, and re-layouts: 60.9 us -> 27.4 us
    dot_general x48 -> x0, matrix products: 511 us -> none  [the longest x4 83.5 us: attend_backward(): jnp.einsum('qhd,khd->hqk', grad_block, value, preferred_element_type=jnp....]
    pallas_call x0 -> x7, Pallas kernels: none -> 272 us  [the longest x1 72.4 us: mlp(): pl.pallas_call(mlp_body, grid=(ff // FC,), in_specs=[whole, whole_t, whol...]
    convert_element_type x32 -> x7, other arithmetic: 110 us -> 7.68 us  [the longest x4 6.91 us: on_device(): grads.append(lax.psum(one, 'dp').astype(F32))]
    reduce_sum x11 -> x0, other arithmetic: 63.6 us -> none  [the longest x4 50.7 us: attend_forward(): total = jnp.sum(exponent, axis=-1, keepdims=True)]
    reduce_scatter x4, waiting for transfers between devices: 167 us -> 222 us  [on_device(): one = lax.psum_scatter(p, 'fsdp', scatter_dimension=0, tiled=True)]
    psum x1, waiting for transfers between devices: 30.7 us -> 0.01 us  [on_device(): grads.append(lax.psum(one, 'dp').astype(F32))]
    unnamed x270 -> x22, local copies, waits for them, and re-layouts: 34.5 us -> 6.35 us
    all_gather x4, waiting for transfers between devices: 0.02 us -> 23.4 us  [on_device(): gather = lambda s: lax.all_gather(s, 'fsdp', axis=0, tiled=True)]
  transfers between devices with their start and end apart: 9 -> 9, of which waited for: 3 -> 4; matrix products, arithmetic and copies ran while one was open for 39% -> 4% of each run, Pallas kernels for 0% -> 26%
where the time goes in v1:
time: 700 us; the launch traced here: 699 us
  Pallas kernels  272 us (39%)
  waiting for transfers between devices  250 us (36%)
  blocking collectives  127 us (18%)
  local copies, waits for them, and re-layouts  27.4 us (4%)
  between operations  14.7 us (2%)
  other arithmetic  8.47 us (1%)
    reduce_scatter x4, waiting for transfers between devices, on_device(): one = lax.psum_scatter(p, 'fsdp', scatter_dimension=0, tiled=True)  222 us
    unnamed x2, blocking collectives  122 us
    pallas_call x1, Pallas kernels, mlp(): pl.pallas_call(mlp_body, grid=(ff // FC,), in_specs=[whole, whole_t, whol...  72.4 us
    pallas_call x1, Pallas kernels, attend(): pl.pallas_call(attend_body, grid=(mb, pairs), in_specs=[pl.BlockSpec((ROW...  64.5 us
    pallas_call x1, Pallas kernels, attend_back(): pl.pallas_call(attend_back_body, grid=(mb, pairs), in_specs=[blk, pl.Bloc...  58.8 us
    pallas_call x1, Pallas kernels, last(): pl.pallas_call(last_body, grid=(rows // tile,), in_specs=[blk, blk, blk,...  34.7 us
    all_gather x4, waiting for transfers between devices, on_device(): gather = lambda s: lax.all_gather(s, 'fsdp', axis=0, tiled=True)  23.4 us
    pallas_call x1, Pallas kernels, middle(): pl.pallas_call(mid_body, grid=(rows // tile,), in_specs=[blk, blk, blk, b...  19.7 us
  transfers between devices with their start and end apart: 9, of which 4 were waited for; matrix products, arithmetic and copies ran while one was open for 4% of the time, Pallas kernels for 26%

profile of v1, /device:TPU:0, one launch (start us, length us, event | category | flops | bytes accessed | tf_op | source)
XLA Modules:
  0.0 699.5 jit_solution(229244213982759699)
XLA Ops:
  7.2 0.7 all-gather.6.cloned.1.call-update
  8.0 0.7 all-gather.8.cloned.1.call-update
  8.7 0.7 all-gather.10.cloned.1.call-update
  9.4 0.5 all-gather.12.cloned.1.call-update
  10.0 1.3 fusion.3
  12.0 6.1 concatenate.20
  18.1 0.2 dynamic-update-slice
  18.3 63.6 %all-reduce = bf16[9216]{0:T(1024)(128)(2,1)S(1)} all-reduce(bf16[9216]{0:T(1024)(128)(2,1)S(1)} %dynamic-update-slice), channel_id=2, replica_groups=mesh['dp'=2,'fsdp'=16] {'fsdp'}, use_global_device_ids=true, to_apply=%add | all-reduce | flops 9216 | bytes 36864
  81.9 0.1 reshape.231
  82.1 0.7 reshape.229.bu_ref
  82.8 0.1 slice_convert_fusion.1
  82.9 0.7 reshape.230.bias_ref
  83.5 0.7 reshape.227.gain_ref
  84.2 0.7 reshape.225.shift_ref
  84.9 0.7 reshape.224.gain_ref
  85.5 0.7 reshape.228.shift_ref
  86.2 0.7 reshape.226.bias_ref
  86.9 0.1 concatenate.22
  87.0 0.1 concatenate.21
  87.1 2.0 copy.36.segc_ref
  89.1 4.7 copy.38
  93.8 0.6 fusion.1.bias_ref
  94.5 13.2 %project.1.q_ref.k_ref.v_ref = bf16[2048,2304]{1,0:T(8,128)(2,1)} custom-call(bf16[2048,768]{1,0:T(8,128)(2,1)} %x_ref.5, f32[1,768]{1,0:T(1,128)} %reshape.224.gain_ref, f32[1,768]{1,0:T(1,128)} %reshape.225.shift_ref, bf16[768,2304]{1,0:T(8,128)(2,1)} %all-gather.6.cloned.1.call-done.w_ref, f32[1,2304]{1,0:T(1,128)} %fusion.1.bias_ref, ...), custom_call_target="tpu_custom_call" | custom-call | flops 7247757312 | bytes 12582912 | tf_op jit(solution)/shard_map/project/pallas_call | solution.py:54
  107.7 64.5 %attend.1 = (bf16[2048,768]{1,0:T(8,128)(2,1)}, bf16[2,12,1024,1024]{3,2,1,0:T(8,128)(2,1)}) custom-call(bf16[2048,2304]{1,0:T(8,128)(2,1)} %project.1.q_ref.k_ref.v_ref, bf16[2048,2304]{1,0:T(8,128)(2,1)} %project.1.q_ref.k_ref.v_ref, bf16[2048,2304]{1,0:T(8,128)(2,1)} %project.1.q_ref.k_ref.v_ref, s32[2048,1]{1,0:T(8,128)} %copy.36.segc_ref, ...), custom_call_target="tpu_custom_call" | custom-call | flops 25769803776 | bytes 50331648 | tf_op jit(solution)/shard_map/attend/pallas_call | solution.py:118
  172.2 8.6 %out_project.1 = (f32[2048,768]{1,0:T(8,128)}, bf16[2048,768]{1,0:T(8,128)(2,1)}) custom-call(bf16[2048,768]{1,0:T(8,128)(2,1)} %x_ref.5, bf16[2048,768]{1,0:T(8,128)(2,1)} %get-tuple-element.41.m_ref.mixed_ref.o_ref, bf16[768,768]{1,0:T(8,128)(2,1)} %all-gather.8.cloned.1.call-done.w_ref, f32[1,768]{1,0:T(1,128)} %reshape.226.bias_ref, ...), custom_call_target="tpu_custom_call" | custom-call | flops 2415919104 | bytes 15728640 | tf_op jit(solution)/shard_map/out_project/pallas_call | solution.py:218
  180.8 4.8 copy.37
  185.6 23.4 %all-gather.12.cloned.1.call-done.wd_ref = bf16[3072,768]{1,0:T(8,128)(2,1)} async-done(((bf16[192,768]{1,0:T(8,128)(2,1)}), bf16[3072,768]{1,0:T(8,128)(2,1)}) %all-gather.12.cloned.1.call-update) | async-done | bytes 4718608 | tf_op jit(solution)/shard_map/all_gather | solution.py:493
  208.9 72.4 %mlp.1 = (f32[2048,768]{1,0:T(8,128)}, f32[2048,768]{1,0:T(8,128)}, bf16[768,3072]{1,0:T(8,128)(2,1)}, bf16[3072,768]{1,0:T(8,128)(2,1)}, f32[1,3072]{1,0:T(1,128)}) custom-call(bf16[2048,768]{1,0:T(8,128)(2,1)} %get-tuple-element.43.h_ref, bf16[768,2048]{1,0:T(8,128)(2,1)} %bitcast.7, bf16[2048,768]{1,0:T(8,128)(2,1)} %g_ref.3, bf16[768,2048]{1,0:T(8,128)(2,1)} %bitcast.6, ...), custom_call_target="tpu_custom_call" | custom-call | flops 57982058496 | bytes 50331648 | tf_op jit(solution)/shard_map/mlp/pallas_call | solution.py:279
  281.4 19.7 %middle.1 = (bf16[2048,768]{1,0:T(8,128)(2,1)}, f32[2048,768]{1,0:T(8,128)}, bf16[2048,768]{1,0:T(8,128)(2,1)}, bf16[768,768]{1,0:T(8,128)(2,1)}, f32[1,768]{1,0...) custom-call(f32[2048,768]{1,0:T(8,128)} %get-tuple-element.42.resid_ref, ...), custom_call_target="tpu_custom_call" | custom-call | flops 4831838208 | bytes 37748736 | tf_op jit(solution)/shard_map/middle/pallas_call | solution.py:371
  301.2 58.8 %attend_back.1 = (bf16[2048,768]{1,0:T(8,128)(2,1)}, bf16[2048,768]{1,0:T(8,128)(2,1)}, bf16[2048,768]{1,0:T(8,128)(2,1)}) custom-call(bf16[2048,2304]{1,0:T(8,128)(2,1)} %project.1.q_ref.k_ref.v_ref, bf16[2048,2304]{1,0:T(8,128)(2,1)} %project.1.q_ref.k_ref.v_ref, bf16[2048,2304]{1,0:T(8,128)(2,1)} %project.1.q_ref.k_ref.v_ref, ...), custom_call_target="tpu_custom_call" | custom-call | flops 51539607552 | bytes 50331648 | tf_op jit(solution)/shard_map/attend_back/pallas_call | solution.py:182
  360.0 34.7 %last.1 = (bf16[2048,768]{1,0:T(8,128)(2,1)}, bf16[768,2304]{1,0:T(8,128)(2,1)}, f32[1,768]{1,0:T(1,128)}, f32[1,768]{1,0:T(1,128)}, f32[1,768]{1,0:T(1,128)}, /*index=5*/f32[1,768]{1,0:T(1,128)}) custom-call(bf16[2048,768]{1,0:T(8,128)(2,1)} %x_ref.5, f32[2048,768]{1,0:T(8,128)} %get-tuple-element.47.dr_ref, bf16[2048,768]{1,0:T(8,128)(2,1)} %get-tuple-element.50.dq_ref, ...), custom_call_target="tpu_custom_call" | custom-call | flops 14495514624 | bytes 22020096 | tf_op jit(solution)/shard_map/last/pallas_call | solution.py:435
  394.7 0.7 reduce-scatter.9.cloned.1.call-update
  395.6 0.7 reduce-scatter.11.cloned.1.call-update
  396.4 65.1 %reduce-scatter.5.cloned.1.call-done = bf16[48,2304]{1,0:T(8,128)(2,1)} async-done(((bf16[768,2304]{1,0:T(8,128)(2,1)}), bf16[48,2304]{1,0:T(8,128)(2,1)}) %reduce-scatter.5.cloned.1.call-update) | async-done | bytes 221200 | tf_op jit(solution)/shard_map/reduce_scatter | solution.py:516
  461.5 78.3 %reduce-scatter.9.cloned.1.call-done = bf16[48,3072]{1,0:T(8,128)(2,1)} async-done(((bf16[768,3072]{1,0:T(8,128)(2,1)}), bf16[48,3072]{1,0:T(8,128)(2,1)}) %reduce-scatter.9.cloned.1.call-update) | async-done | bytes 294928 | tf_op jit(solution)/shard_map/reduce_scatter | solution.py:516
  539.8 79.0 %reduce-scatter.11.cloned.1.call-done = bf16[192,768]{1,0:T(8,128)(2,1)} async-done(((bf16[3072,768]{1,0:T(8,128)(2,1)}), bf16[192,768]{1,0:T(8,128)(2,1)}) %reduce-scatter.11.cloned.1.call-update) | async-done | bytes 294928 | tf_op jit(solution)/shard_map/reduce_scatter | solution.py:516
  619.6 0.5 broadcast.21
  620.2 0.7 reduce.13
  620.9 0.1 concatenate.24
  621.0 58.1 %all-reduce.1 = f32[16,576]{1,0:T(8,128)S(1)} all-reduce(f32[16,576]{1,0:T(8,128)S(1)} %concatenate.24), channel_id=3, replica_groups=mesh['dp'=2,'fsdp'=16] {'fsdp'}, use_global_device_ids=true, to_apply=%region_0.0.clone | all-reduce | flops 9216 | bytes 73728
  679.2 0.7 dynamic-slice_reduce_fusion
  679.8 4.9 psum.35
  684.8 0.6 slice.70
  685.4 0.6 fusion.2
  686.0 1.6 convert_element_type.132
  687.6 1.7 convert_element_type.131
  689.3 1.8 convert_element_type.133
  691.1 1.8 convert_element_type.134
  (56 shorter events, 1.3 us)
Async XLA Ops:
  7.2 87.3 %all-gather.6.cloned.1.call-start = ((), (), s32[]{:S(2)}) async-start(), calls=%async_computation.4 | async-start | bytes 3760128 | tf_op jit(solution)/shard_map/all_gather | solution.py:493
  7.9 164.3 %all-gather.8.cloned.1.call-start = ((), (), s32[]{:S(2)}) async-start(), calls=%async_computation.5 | async-start | bytes 1253376 | tf_op jit(solution)/shard_map/all_gather | solution.py:493
  8.7 176.9 %all-gather.10.cloned.1.call-start = ((), (), s32[]{:S(2)}) async-start(), calls=%async_computation.6 | async-start | bytes 5013504 | tf_op jit(solution)/shard_map/all_gather | solution.py:493
  9.4 199.5 %all-gather.12.cloned.1.call-start = ((), (), s32[]{:S(2)}) async-start(), calls=%async_computation.7 | async-start | bytes 5013504 | tf_op jit(solution)/shard_map/all_gather | solution.py:493
  10.0 386.4 %reduce-scatter.7.cloned.1.call-start = ((), (), s32[]{:S(2)}) async-start(), calls=%async_computation.9 | async-start | bytes 1253376 | tf_op jit(solution)/shard_map/reduce_scatter | solution.py:516
  301.1 160.4 %reduce-scatter.5.cloned.1.call-start = ((), (), s32[]{:S(2)}) async-start(), calls=%async_computation.8 | async-start | bytes 3760128 | tf_op jit(solution)/shard_map/reduce_scatter | solution.py:516
  394.7 145.1 %reduce-scatter.9.cloned.1.call-start = ((), (), s32[]{:S(2)}) async-start(), calls=%async_computation.10 | async-start | bytes 5013504 | tf_op jit(solution)/shard_map/reduce_scatter | solution.py:516
  395.4 223.4 %copy-start.8 = (f32[1,768]{1,0:T(1,128)S(1)}, f32[1,768]{1,0:T(1,128)}, u32[]{:S(2)}) copy-start(f32[1,768]{1,0:T(1,128)} %get-tuple-element.54) | copy-start | bytes 9220
  395.4 223.5 %copy-start.7 = (f32[1,768]{1,0:T(1,128)S(1)}, f32[1,768]{1,0:T(1,128)}, u32[]{:S(2)}) copy-start(f32[1,768]{1,0:T(1,128)} %get-tuple-element.55) | copy-start | bytes 9220
  395.5 223.6 %copy-start.6 = (f32[1,768]{1,0:T(1,128)S(1)}, f32[1,768]{1,0:T(1,128)}, u32[]{:S(2)}) copy-start(f32[1,768]{1,0:T(1,128)} %get-tuple-element.56) | copy-start | bytes 9220
  395.5 223.7 %copy-start.5 = (f32[1,768]{1,0:T(1,128)S(1)}, f32[1,768]{1,0:T(1,128)}, u32[]{:S(2)}) copy-start(f32[1,768]{1,0:T(1,128)} %get-tuple-element.57) | copy-start | bytes 9220
  395.5 223.8 %copy-start.4 = (f32[1,768]{1,0:T(1,128)S(1)}, f32[1,768]{1,0:T(1,128)}, u32[]{:S(2)}) copy-start(f32[1,768]{1,0:T(1,128)} %get-tuple-element.58) | copy-start | bytes 9220
  395.5 223.9 %copy-start.3 = (f32[1,768]{1,0:T(1,128)S(1)}, f32[1,768]{1,0:T(1,128)}, u32[]{:S(2)}) copy-start(f32[1,768]{1,0:T(1,128)} %get-tuple-element.59) | copy-start | bytes 9220
  395.5 223.9 %copy-start.2 = (f32[1,768]{1,0:T(1,128)S(1)}, f32[1,768]{1,0:T(1,128)}, u32[]{:S(2)}) copy-start(f32[1,768]{1,0:T(1,128)} %get-tuple-element.60) | copy-start | bytes 9220
  395.5 224.0 %copy-start.1 = (f32[1,768]{1,0:T(1,128)S(1)}, f32[1,768]{1,0:T(1,128)}, u32[]{:S(2)}) copy-start(f32[1,768]{1,0:T(1,128)} %get-tuple-element.62) | copy-start | bytes 9220
  395.5 224.6 %copy-start = (f32[1,3072]{1,0:T(1,128)S(1)}, f32[1,3072]{1,0:T(1,128)}, u32[]{:S(2)}) copy-start(f32[1,3072]{1,0:T(1,128)} %get-tuple-element.61) | copy-start | bytes 36868
  395.5 223.3 %reduce-scatter.11.cloned.1.call-start = ((), (), s32[]{:S(2)}) async-start(), calls=%async_computation.11 | async-start | bytes 5013504 | tf_op jit(solution)/shard_map/reduce_scatter | solution.py:516
  396.3 289.7 %all-reduce.5.cloned.1.call-start = ((), (), s32[]{:S(2)}) async-start(), calls=%async_computation.12 | async-start | bytes 1769472 | tf_op jit(solution)/shard_map/psum | solution.py:517
Sparse Core Ops, SparseCore 0:
  10.3 50.3 all-gather.5
  63.0 37.4 all-gather.7
  102.8 52.2 all-gather.9
  157.2 51.7 all-gather.11
  301.3 56.6 reduce-scatter.6
  394.8 66.6 reduce-scatter.4
  465.4 74.4 reduce-scatter.8
  544.2 74.6 reduce-scatter.10
  621.3 36.0 all-reduce.4
